TPU v7x, 32 devices: a whole 2x2x4 slice. The times are simulated.
32 devices in a mesh: rows: 8 (over z, y), cols: 4 (over x, core).
Axes of the slice: x: 2, y: 2, z: 4, core: 2. Of those that a mesh axis runs over, the one named last changes fastest.
Arguments:
- right_leaf: float32 [4, 2048, 128], P(None, 'rows'), may hold values from -6 to 6
- right_mid: float32 [2, 4096, 128], P(None, 'rows'), may hold values from -6 to 6
- right_root: float32 [8192, 128], P('rows'), may hold values from -6 to 6
- inverse_leaf: float32 [4, 2048, 2048], P(None, 'rows', 'cols'), may hold values from -1 to 2, as said below
- inverse_mid: float32 [2, 4096, 4096], P(None, 'rows', 'cols'), may hold values from -1 to 2, as said below
- inverse_root: float32 [8192, 8192], P('rows', 'cols'), may hold values from -1 to 2, as said below
- leaf_to_mid: float32 [4, 4096, 2048], P(None, 'rows', 'cols'), may hold values from -0.125 to 0.125
- leaf_to_root: float32 [4, 8192, 2048], P(None, 'rows', 'cols'), may hold values from -0.125 to 0.125
- mid_to_root: float32 [2, 8192, 4096], P(None, 'rows', 'cols'), may hold values from -0.09375 to 0.09375
- mask_leaf_mid: int32 [4, 32, 16], replicated, may hold values 0 or 1
- mask_leaf_root: int32 [4, 64, 16], replicated, may hold values 0 or 1
- mask_mid_root: int32 [2, 64, 32], replicated, may hold values 0 or 1
Outputs:
- solved_leaf: float32 [4, 2048, 128], P(None, 'rows')
- solved_mid: float32 [2, 4096, 128], P(None, 'rows')
- solved_root: float32 [8192, 128], P('rows')
Inputs may be any that keep to these rules, and one draw needn't show every extreme that they name: `inverse_leaf`: lower triangular, with its diagonal between 0.5 and 2. `inverse_mid`: lower triangular, with its diagonal between 0.5 and 2. `inverse_root`: lower triangular, with its diagonal between 0.5 and 2.
All inputs are finite; a program needn't handle non-finite values.
Results may differ from a plain program's by a relative error of at most 0.00014.
Values sent between devices are 32-bit elements; how exact they have to be, the bound alone decides.
No kernel may reach another device: no remote copies, remote signals or barrier semaphores. Data moves between devices by JAX's collectives and lax.ppermute only.
A program may use at most 128 MiB of HBM per device.

v0:
```python
import jax
import jax.numpy as jnp
from jax import lax
from jax.sharding import PartitionSpec as P

TILE = 128


def product(matrix, vector):
    return jnp.einsum(
        "src,sck->srk",
        matrix,
        vector,
        precision=lax.Precision.HIGHEST,
        preferred_element_type=jnp.float32,
    )


def own_columns(gathered):
    col_width = gathered.shape[1] // lax.axis_size("cols")
    return lax.dynamic_slice_in_dim(gathered, lax.axis_index("cols") * col_width, col_width, 1)


def masked(values, pattern):
    rows_dev = values.shape[1]
    cols_dev = values.shape[2]
    row_ids = lax.axis_index("rows") * rows_dev + lax.iota(jnp.int32, rows_dev)
    col_ids = lax.axis_index("cols") * cols_dev + lax.iota(jnp.int32, cols_dev)
    row_hot = (row_ids[:, None] // TILE == lax.iota(jnp.int32, pattern.shape[1])[None, :]).astype(
        jnp.float32
    )
    col_hot = (col_ids[:, None] // TILE == lax.iota(jnp.int32, pattern.shape[2])[None, :]).astype(
        jnp.float32
    )
    expanded = jnp.einsum("ra,sab,cb->src", row_hot, pattern.astype(jnp.float32), col_hot)
    return values * expanded


def fetch_columns(block):
    gathered = lax.all_gather(block, "rows", axis=1, tiled=True)
    return own_columns(gathered)


def solve_block(residual, inverse, spread_needed):
    partial_value = product(inverse, fetch_columns(residual))
    solved = lax.psum(partial_value, "cols")
    spread = fetch_columns(solved) if spread_needed else solved
    return (solved, spread)


def body(
    right_leaf,
    right_mid,
    right_root,
    inverse_leaf,
    inverse_mid,
    inverse_root,
    leaf_to_mid,
    leaf_to_root,
    mid_to_root,
    mask_leaf_mid,
    mask_leaf_root,
    mask_mid_root,
):
    factor_lm = masked(leaf_to_mid, mask_leaf_mid)
    factor_lr = masked(leaf_to_root, mask_leaf_root)
    factor_mr = masked(mid_to_root, mask_mid_root)
    solved_leaf, leaf_columns = solve_block(right_leaf, inverse_leaf, True)
    mid_terms = product(factor_lm, leaf_columns)
    mid_part = mid_terms.reshape(2, 2, mid_terms.shape[1], mid_terms.shape[2]).sum(axis=1)
    root_part = product(factor_lr, leaf_columns).sum(axis=0)[None]
    mid_summed, root_summed = lax.psum((mid_part, root_part), "cols")
    resid_mid = right_mid - mid_summed
    solved_mid, mid_columns = solve_block(resid_mid, inverse_mid, True)
    root_more = product(factor_mr, mid_columns).sum(axis=0)[None]
    resid_root = right_root[None] - root_summed - lax.psum(root_more, "cols")
    solved_root, unused_spread = solve_block(resid_root, inverse_root[None], False)
    return (solved_leaf, solved_mid, solved_root[0])


def solution(mesh):
    placed = (
        P(None, "rows", None),
        P(None, "rows", None),
        P("rows", None),
        P(None, "rows", "cols"),
        P(None, "rows", "cols"),
        P("rows", "cols"),
        P(None, "rows", "cols"),
        P(None, "rows", "cols"),
        P(None, "rows", "cols"),
        P(),
        P(),
        P(),
    )
    return jax.shard_map(
        body,
        mesh=mesh,
        in_specs=placed,
        out_specs=(P(None, "rows", None), P(None, "rows", None), P("rows", None)),
        check_vma=False,
    )
```

profile of v0, /device:TPU:0, one launch (start us, length us, event | category | flops | bytes accessed | tf_op | source)
XLA Modules:
  0.0 608.7 jit_solution(15092546820964897420)
XLA Ops:
  7.2 0.0 copy-start
  7.2 0.0 copy-start.6
  7.2 0.0 all-gather.6.cloned.1.call-start
  7.2 2.2 copy.32
  9.4 0.0 all-gather.6.cloned.1.call-update
  9.4 0.0 all-reduce.7.cloned.1.call-start
  9.5 78.9 %all-gather.6.cloned.1.call-done = f32[4,2048,128]{1,2,0:T(8,128)} async-done(((f32[4,256,128]{1,2,0:T(8,128)}), f32[4,2048,128]{1,2,0:T(8,128)}) %all-gather.6.cloned.1.call-update) | async-done | bytes 4194320 | tf_op jit(solution)/shard_map/all_gather | solution.py:40
  88.4 0.0 copy-done
  88.4 4.2 convolution_bitcast_fusion.1
  92.6 0.0 all-reduce.7.cloned.1.call-update
  92.6 0.0 all-gather.8.cloned.1.call-start
  92.7 31.4 %all-reduce.7.cloned.1.call-done = f32[4,256,128]{1,2,0:T(8,128)} async-done(((f32[4,256,128]{1,2,0:T(8,128)}), f32[4,256,128]{1,2,0:T(8,128)}) %all-reduce.7.cloned.1.call-update) | async-done | bytes 524304 | tf_op jit(solution)/shard_map/psum | solution.py:46
  124.1 0.0 all-gather.8.cloned.1.call-update
  124.1 0.0 all-reduce.9.cloned.1.call-start
  124.2 0.0 copy-done.6
  124.3 0.2 fusion.32
  124.4 2.7 fusion.37
  127.1 74.1 %all-gather.8.cloned.1.call-done = f32[4,2048,128]{1,2,0:T(8,128)} async-done(((f32[4,256,128]{1,2,0:T(8,128)}), f32[4,2048,128]{1,2,0:T(8,128)}) %all-gather.8.cloned.1.call-update) | async-done | bytes 4194320 | tf_op jit(solution)/shard_map/all_gather | solution.py:40
  201.2 7.5 %bitcast_reduce_fusion = f32[2,512,128]{2,1,0:T(8,128)S(1)} fusion(f32[4,2048,128]{1,2,0:T(8,128)} %all-gather.8.cloned.1.call-done, s32[]{:T(128)S(6)} %select_n.49, f32[4,512,512]{2,1,0:T(8,128)} %param.18, f32[4,512,512]{2,1,0:T(8,128)} %fusion.37), kind=kOutput, calls=%fused_computation.12 | convolution fusion | flops 1611792384 | bytes 9961476 | tf_op jit(solution)/shard_map/src,sck->srk/dot_general | solution.py:10
  208.7 1.0 copy.34
  209.7 0.0 all-reduce.9.cloned.1.call-update
  209.7 0.0 all-gather.10.cloned.1.call-start
  209.8 0.0 copy-done.4
  209.8 0.2 copy.35
  210.0 0.0 copy-start.7
  210.0 0.0 copy-start.8
  210.0 31.2 %all-reduce.9.cloned.1.call-done = f32[2,512,128]{1,2,0:T(8,128)} async-done(((f32[2,512,128]{1,2,0:T(8,128)}), f32[2,512,128]{1,2,0:T(8,128)}) %all-reduce.9.cloned.1.call-update) | async-done | bytes 524304 | tf_op jit(solution)/shard_map/psum | solution.py:72
  241.3 1.9 sub.35
  243.2 0.0 all-gather.10.cloned.1.call-update
  243.2 0.0 all-reduce.11.cloned.1.call-start
  243.3 74.0 %all-gather.10.cloned.1.call-done = f32[2,4096,128]{1,2,0:T(8,128)} async-done(((f32[2,512,128]{1,2,0:T(8,128)}), f32[2,4096,128]{1,2,0:T(8,128)}) %all-gather.10.cloned.1.call-update) | async-done | bytes 4194320 | tf_op jit(solution)/shard_map/all_gather | solution.py:40
  317.3 7.7 %convolution_bitcast_fusion.2 = f32[2,512,128]{1,2,0:T(8,128)} fusion(f32[2,512,1024]{2,1,0:T(8,128)} %param.16, f32[2,4096,128]{1,2,0:T(8,128)} %all-gather.10.cloned.1.call-done, s32[]{:T(128)S(6)} %select_n.52), kind=kOutput, calls=%fused_computation.10 | convolution fusion | flops 1610612736 | bytes 5767172 | tf_op jit(solution)/shard_map/src,sck->srk/dot_general | solution.py:10
  325.0 0.0 all-reduce.11.cloned.1.call-update
  325.0 0.0 all-gather.12.cloned.1.call-start
  325.0 31.5 %all-reduce.11.cloned.1.call-done = f32[2,512,128]{1,2,0:T(8,128)} async-done(((f32[2,512,128]{1,2,0:T(8,128)}), f32[2,512,128]{1,2,0:T(8,128)}) %all-reduce.11.cloned.1.call-update) | async-done | bytes 524304 | tf_op jit(solution)/shard_map/psum | solution.py:46
  356.6 0.0 all-gather.12.cloned.1.call-update
  356.6 0.2 all-reduce.15.cloned.1.call-start
  356.8 0.0 copy-done.7
  356.9 0.0 copy-done.8
  356.9 0.2 fusion.24
  357.1 0.2 fusion.25
  357.3 0.0 slice-start
  357.3 1.3 fusion.35
  358.6 0.0 slice-start.1
  358.6 4.5 fusion.29
  363.1 0.0 slice-done
  363.1 8.7 %fusion.6 = f32[1,1024,128]{2,1,0:T(8,128)} fusion(f32[4,1024,512]{2,1,0:T(8,128)S(1)} %bitcast.56, f32[4,1024,512]{2,1,0:T(8,128)S(1)} %fusion.35, f32[4,2048,128]{1,2,0:T(8,128)} %all-gather.8.cloned.1.call-done, s32[]{:T(128)S(6)} %select_n.49), kind=kOutput, calls=%fused_computation.6 | convolution fusion | flops 3223322624 | bytes 18350084 | tf_op jit(solution)/shard_map/src,sck->srk/dot_general | solution.py:10
  371.9 60.3 %all-gather.12.cloned.1.call-done = f32[2,4096,128]{1,2,0:T(8,128)} async-done(((f32[2,512,128]{1,2,0:T(8,128)}), f32[2,4096,128]{1,2,0:T(8,128)}) %all-gather.12.cloned.1.call-update) | async-done | bytes 4194320 | tf_op jit(solution)/shard_map/all_gather | solution.py:40
  432.2 11.2 %fusion.9 = f32[1,1024,128]{2,1,0:T(8,128)} fusion(f32[2,1024,1024]{2,1,0:T(8,128)} %param.20, f32[2,1024,1024]{2,1,0:T(8,128)} %fusion.29, f32[2,4096,128]{1,2,0:T(8,128)} %all-gather.12.cloned.1.call-done, s32[]{:T(128)S(6)} %select_n.52), kind=kOutput, calls=%fused_computation.7 | convolution fusion | flops 3223322624 | bytes 18350084 | tf_op jit(solution)/shard_map/src,sck->srk/dot_general | solution.py:10
  443.4 0.0 all-reduce.15.cloned.1.call-update
  443.5 0.0 all-gather.14.cloned.1.call-start
  443.5 34.5 %all-reduce.15.cloned.1.call-done = (f32[1,1024,128]{2,1,0:T(8,128)}, f32[1,1024,128]{2,1,0:T(8,128)}) async-done(((f32[1,1024,128]{2,1,0:T(8,128)}, f32[1,1024,128]{2,1,0:T(8,128)}), (f32[1,1024,128]{2,1,0:T(8,128)}, f32[1,1024,128]{2,1,0:T(8,128)})) %all-reduce.15.cloned.1.call-update) | async-done | bytes 1048592 | tf_op jit(solution)/shard_map/psum | solution.py:76
  478.1 0.0 copy-done.5
  478.1 2.1 fusion.23
  480.1 0.0 all-gather.14.cloned.1.call-update
  480.2 0.0 all-reduce.13.cloned.1.call-start
  480.2 74.6 %all-gather.14.cloned.1.call-done = f32[1,8192,128]{2,1,0:T(8,128)} async-done(((f32[1,1024,128]{2,1,0:T(8,128)}), f32[1,8192,128]{2,1,0:T(8,128)}) %all-gather.14.cloned.1.call-update) | async-done | bytes 4194320 | tf_op jit(solution)/shard_map/all_gather | solution.py:40
  554.8 13.4 %convolution_bitcast_fusion = f32[1024,128]{0,1:T(8,128)} fusion(f32[1024,2048]{1,0:T(8,128)} %param.17, f32[1,8192,128]{2,1,0:T(8,128)} %all-gather.14.cloned.1.call-done, s32[]{:T(128)S(6)} %select_n.55), kind=kOutput, calls=%fused_computation.8 | convolution fusion | flops 3221225472 | bytes 9961476 | tf_op jit(solution)/shard_map/src,sck->srk/dot_general | solution.py:10
  568.3 0.0 all-reduce.13.cloned.1.call-update
  568.3 1.0 copy.38
  569.3 1.0 copy.39
  570.3 29.6 %all-reduce.13.cloned.1.call-done = f32[1024,128]{0,1:T(8,128)} async-done(((f32[1024,128]{0,1:T(8,128)}), f32[1024,128]{0,1:T(8,128)}) %all-reduce.13.cloned.1.call-update) | async-done | bytes 524304 | tf_op jit(solution)/shard_map/psum | solution.py:46
  599.9 2.0 copy.40
  601.9 0.0 copy-done.1
  (16 shorter events, 0.1 us)
Async XLA Ops:
  7.2 81.2 %copy-start = (f32[4,256,512]{2,1,0:T(8,128)S(1)}, f32[4,256,512]{2,1,0:T(8,128)}, u32[]{:S(2)}) copy-start(f32[4,256,512]{2,1,0:T(8,128)} %param.15) | copy-start | bytes 6291460
  7.2 117.0 %copy-start.6 = (s32[4,32,16]{1,2,0:T(8,128)S(1)}, s32[4,32,16]{1,2,0:T(8,128)}, u32[]{:S(2)}) copy-start(s32[4,32,16]{1,2,0:T(8,128)} %param.21) | copy-start | bytes 24580
  7.2 81.2 %all-gather.6.cloned.1.call-start = ((), (), s32[]{:S(2)}) async-start(), calls=%async_computation | async-start | bytes 4718592 | tf_op jit(solution)/shard_map/all_gather | solution.py:40
  9.4 114.7 %all-reduce.7.cloned.1.call-start = ((), (), s32[]{:S(2)}) async-start(), calls=%async_computation.1 | async-start | bytes 1048576 | tf_op jit(solution)/shard_map/psum | solution.py:46
  92.6 108.6 %all-gather.8.cloned.1.call-start = ((), (), s32[]{:S(2)}) async-start(), calls=%async_computation.2 | async-start | bytes 4718592 | tf_op jit(solution)/shard_map/all_gather | solution.py:40
  124.1 117.1 %all-reduce.9.cloned.1.call-start = ((), (), s32[]{:S(2)}) async-start(), calls=%async_computation.3 | async-start | bytes 1048576 | tf_op jit(solution)/shard_map/psum | solution.py:72
  127.1 82.7 %copy-start.4 = (f32[2,512,128]{2,1,0:T(8,128)S(1)}, f32[2,512,128]{2,1,0:T(8,128)}, u32[]{:S(2)}) copy-start(f32[2,512,128]{2,1,0:T(8,128)} %param.13) | copy-start | bytes 1572868
  209.7 107.5 %all-gather.10.cloned.1.call-start = ((), (), s32[]{:S(2)}) async-start(), calls=%async_computation.4 | async-start | bytes 4718592 | tf_op jit(solution)/shard_map/all_gather | solution.py:40
  210.0 146.8 %copy-start.7 = (s32[2,64,32]{1,2,0:T(8,128)S(1)}, s32[2,64,32]{1,2,0:T(8,128)}, u32[]{:S(2)}) copy-start(s32[2,64,32]{1,2,0:T(8,128)} %param.23) | copy-start | bytes 49156
  210.0 146.8 %copy-start.8 = (s32[4,64,16]{1,2,0:T(8,128)S(1)}, s32[4,64,16]{1,2,0:T(8,128)}, u32[]{:S(2)}) copy-start(s32[4,64,16]{1,2,0:T(8,128)} %param.22) | copy-start | bytes 49156
  243.2 113.4 %all-reduce.11.cloned.1.call-start = ((), (), s32[]{:S(2)}) async-start(), calls=%async_computation.5 | async-start | bytes 1048576 | tf_op jit(solution)/shard_map/psum | solution.py:46
  325.0 107.2 %all-gather.12.cloned.1.call-start = ((), (), s32[]{:S(2)}) async-start(), calls=%async_computation.6 | async-start | bytes 4718592 | tf_op jit(solution)/shard_map/all_gather | solution.py:40
  356.6 121.5 %all-reduce.15.cloned.1.call-start = ((), (), s32[]{:S(2)}) async-start(), calls=%async_computation.9 | async-start | bytes 2097152 | tf_op jit(solution)/shard_map/psum | solution.py:76
  357.3 5.8 slice-start
  358.6 4.6 slice-start.1
  371.9 106.2 %copy-start.5 = (f32[1024,128]{1,0:T(8,128)S(1)}, f32[1024,128]{1,0:T(8,128)}, u32[]{:S(2)}) copy-start(f32[1024,128]{1,0:T(8,128)} %param.14) | copy-start | bytes 1572868
  443.5 111.4 %all-gather.14.cloned.1.call-start = ((), (), s32[]{:S(2)}) async-start(), calls=%async_computation.7 | async-start | bytes 4718592 | tf_op jit(solution)/shard_map/all_gather | solution.py:40
  480.2 119.7 %all-reduce.13.cloned.1.call-start = ((), (), s32[]{:S(2)}) async-start(), calls=%async_computation.8 | async-start | bytes 1048576 | tf_op jit(solution)/shard_map/psum | solution.py:46
  480.2 88.1 %copy-start.2 = (f32[4,256,128]{1,2,0:T(8,128)S(1)}, f32[4,256,128]{1,2,0:T(8,128)}, u32[]{:S(2)}) copy-start(f32[4,256,128]{1,2,0:T(8,128)} %all-reduce.7.cloned.1.call-done) | copy-start | bytes 1572868
  480.2 89.1 %copy-start.3 = (f32[2,512,128]{1,2,0:T(8,128)S(1)}, f32[2,512,128]{1,2,0:T(8,128)}, u32[]{:S(2)}) copy-start(f32[2,512,128]{1,2,0:T(8,128)} %all-reduce.11.cloned.1.call-done) | copy-start | bytes 1572868
  554.8 47.1 %copy-start.1 = (f32[4,256,512]{2,1,0:T(8,128)S(1)}, f32[4,256,512]{2,1,0:T(8,128)}, u32[]{:S(2)}) copy-start(f32[4,256,512]{2,1,0:T(8,128)} %param.15) | copy-start | bytes 6291460
Sparse Core Ops, SparseCore 0:
  10.6 77.7 all-gather.5
  92.8 31.3 all-reduce.6
  126.2 75.0 all-gather.7
  209.9 31.3 all-reduce.8
  243.9 73.3 all-gather.9
  325.1 31.4 all-reduce.10
  358.8 73.3 all-gather.11
  443.6 34.4 all-reduce.14
  481.0 73.8 all-gather.13
  568.4 31.4 all-reduce.12
where the time goes:
time: 609 us
  waiting for transfers between devices  520 us (85%)
  matrix products  61.8 us (10%)
  between operations  14.4 us (2%)
  local copies, waits for them, and re-layouts  7.45 us (1%)
    all_gather x5, waiting for transfers between devices, fetch_columns(): gathered = lax.all_gather(block, 'rows', axis=1, tiled=True)  362 us
    psum x3, waiting for transfers between devices, solve_block(): solved = lax.psum(partial_value, 'cols')  92.6 us
    dot_general x6, matrix products, product(): jnp.einsum('src,sck->srk', matrix, vector, precision=lax.Precision.HIGHES...  52.8 us
    psum x1, waiting for transfers between devices, body(): resid_root = right_root[None] - root_summed - lax.psum(root_more, 'cols')  34.5 us
    psum x1, waiting for transfers between devices, body(): mid_summed, root_summed = lax.psum((mid_part, root_part), 'cols')  31.2 us
  transfers between devices with their start and end apart: 10, of which 10 were waited for; matrix products, arithmetic and copies ran while one was open for 3% of the time, Pallas kernels for 0%

commit v1 on v0

--- a/solution.py
+++ b/solution.py
@@ -43,7 +43,7 @@
 
 def solve_block(residual, inverse, spread_needed):
     partial_value = product(inverse, fetch_columns(residual))
-    solved = lax.psum(partial_value, "cols")
+    solved = jnp.sum(lax.all_gather(partial_value, "cols"), axis=0)
     spread = fetch_columns(solved) if spread_needed else solved
     return (solved, spread)
 

time: 609 us -> 593 us (0.974); the launches traced: 609 us -> 585 us
  waiting for transfers between devices: 520 us -> 485 us
  other arithmetic: 4.05 us -> 12 us
    psum x3 -> x0, waiting for transfers between devices: 92.6 us -> none  [solve_block(): solved = lax.psum(partial_value, 'cols')]
    all_gather x0 -> x3, waiting for transfers between devices: none -> 62.8 us  [solve_block(): solved = jnp.sum(lax.all_gather(partial_value, 'cols'), axis=0)]
    reduce_sum x0 -> x3, other arithmetic: none -> 7.96 us  [solve_block(): solved = jnp.sum(lax.all_gather(partial_value, 'cols'), axis=0)]
where the time goes in v1:
time: 593 us; the launch traced here: 585 us
  waiting for transfers between devices  485 us (82%)
  matrix products  62.5 us (11%)
  between operations  14.8 us (2%)
  other arithmetic  12 us (2%)
  local copies, waits for them, and re-layouts  10 us (2%)
    all_gather x5, waiting for transfers between devices, fetch_columns(): gathered = lax.all_gather(block, 'rows', axis=1, tiled=True)  356 us
    all_gather x3, waiting for transfers between devices, solve_block(): solved = jnp.sum(lax.all_gather(partial_value, 'cols'), axis=0)  62.8 us
    dot_general x6, matrix products, product(): jnp.einsum('src,sck->srk', matrix, vector, precision=lax.Precision.HIGHES...  53.5 us
    psum x1, waiting for transfers between devices, body(): resid_root = right_root[None] - root_summed - lax.psum(root_more, 'cols')  34.5 us
    psum x1, waiting for transfers between devices, body(): mid_summed, root_summed = lax.psum((mid_part, root_part), 'cols')  31.3 us
  transfers between devices with their start and end apart: 10, of which 10 were waited for; matrix products, arithmetic and copies ran while one was open for 3% of the time, Pallas kernels for 0%

profile of v1, /device:TPU:0, one launch (start us, length us, event | category | flops | bytes accessed | tf_op | source)
XLA Modules:
  0.0 585.2 jit_solution(12179802856103665473)
XLA Ops:
  7.2 0.0 copy-start
  7.2 0.0 all-gather.12.cloned.1.call-start
  7.2 2.2 copy.29
  9.4 0.0 all-gather.12.cloned.1.call-update
  9.4 0.0 all-gather.22.cloned.1.call-start
  9.5 0.0 copy-start.4
  9.5 78.9 %all-gather.12.cloned.1.call-done = f32[4,2048,128]{1,2,0:T(8,128)} async-done(((f32[4,256,128]{1,2,0:T(8,128)}), f32[4,2048,128]{1,2,0:T(8,128)}) %all-gather.12.cloned.1.call-update) | async-done | bytes 4194320 | tf_op jit(solution)/shard_map/all_gather | solution.py:40
  88.4 0.0 copy-done
  88.4 3.4 convolution_bitcast_fusion.1
  91.8 1.0 copy.30
  92.8 0.0 all-gather.22.cloned.1.call-update
  92.8 0.0 all-gather.14.cloned.1.call-start
  92.9 20.9 %all-gather.22.cloned.1.call-done = f32[16,256,128]{2,1,0:T(8,128)} async-done(((f32[4,256,128]{2,1,0:T(8,128)}), f32[16,256,128]{2,1,0:T(8,128)}) %all-gather.22.cloned.1.call-update) | async-done | bytes 2097168 | tf_op jit(solution)/shard_map/all_gather | solution.py:46
  113.7 2.5 reduce_sum.35
  116.3 0.0 all-gather.14.cloned.1.call-update
  116.3 0.0 all-reduce.4.cloned.1.call-start
  116.4 0.2 fusion.32
  116.6 2.7 fusion.37
  119.3 70.7 %all-gather.14.cloned.1.call-done = f32[4,2048,128]{2,1,0:T(8,128)} async-done(((f32[4,256,128]{2,1,0:T(8,128)}), f32[4,2048,128]{2,1,0:T(8,128)}) %all-gather.14.cloned.1.call-update) | async-done | bytes 4194320 | tf_op jit(solution)/shard_map/all_gather | solution.py:40
  189.9 7.5 %bitcast_reduce_fusion = f32[2,512,128]{2,1,0:T(8,128)S(1)} fusion(f32[4,2048,128]{2,1,0:T(8,128)} %all-gather.14.cloned.1.call-done, s32[]{:T(128)S(6)} %select_n.49, f32[4,512,512]{2,1,0:T(8,128)} %param.18, f32[4,512,512]{2,1,0:T(8,128)} %fusion.37), kind=kOutput, calls=%fused_computation.12 | convolution fusion | flops 1611792384 | bytes 9961476 | tf_op jit(solution)/shard_map/src,sck->srk/dot_general | solution.py:10
  197.4 1.0 copy.33
  198.4 0.0 all-reduce.4.cloned.1.call-update
  198.4 0.0 all-gather.16.cloned.1.call-start
  198.5 0.2 copy.34
  198.7 31.3 %all-reduce.4.cloned.1.call-done = f32[2,512,128]{1,2,0:T(8,128)} async-done(((f32[2,512,128]{1,2,0:T(8,128)}), f32[2,512,128]{1,2,0:T(8,128)}) %all-reduce.4.cloned.1.call-update) | async-done | bytes 524304 | tf_op jit(solution)/shard_map/psum | solution.py:72
  230.0 1.9 sub.35
  232.0 0.0 all-gather.16.cloned.1.call-update
  232.0 0.0 all-gather.24.cloned.1.call-start
  232.0 0.0 copy-start.5
  232.0 0.0 copy-start.6
  232.1 74.0 %all-gather.16.cloned.1.call-done = f32[2,4096,128]{1,2,0:T(8,128)} async-done(((f32[2,512,128]{1,2,0:T(8,128)}), f32[2,4096,128]{1,2,0:T(8,128)}) %all-gather.16.cloned.1.call-update) | async-done | bytes 4194320 | tf_op jit(solution)/shard_map/all_gather | solution.py:40
  306.1 6.9 %convolution_bitcast_fusion.2 = f32[2,512,128]{1,2,0:T(8,128)S(1)} fusion(f32[2,512,1024]{2,1,0:T(8,128)} %param.16, f32[2,4096,128]{1,2,0:T(8,128)} %all-gather.16.cloned.1.call-done, s32[]{:T(128)S(6)} %select_n.52), kind=kOutput, calls=%fused_computation.10 | convolution fusion | flops 1610612736 | bytes 5767172 | tf_op jit(solution)/shard_map/src,sck->srk/dot_general | solution.py:10
  312.9 1.0 copy.35
  313.9 0.0 all-gather.24.cloned.1.call-update
  314.0 0.0 all-gather.18.cloned.1.call-start
  314.0 21.0 %all-gather.24.cloned.1.call-done = f32[8,512,128]{2,1,0:T(8,128)} async-done(((f32[2,512,128]{2,1,0:T(8,128)}), f32[8,512,128]{2,1,0:T(8,128)}) %all-gather.24.cloned.1.call-update) | async-done | bytes 2097168 | tf_op jit(solution)/shard_map/all_gather | solution.py:46
  335.0 2.5 reduce_sum.37
  337.5 0.0 all-gather.18.cloned.1.call-update
  337.6 0.2 all-reduce.6.cloned.1.call-start
  337.9 0.2 fusion.24
  338.0 0.2 fusion.25
  338.2 0.0 slice-start
  338.3 1.3 fusion.35
  339.5 0.0 slice-start.1
  339.5 4.5 fusion.29
  344.1 0.0 slice-done
  344.1 8.8 %fusion.6 = f32[1,1024,128]{2,1,0:T(8,128)} fusion(f32[4,1024,512]{2,1,0:T(8,128)S(1)} %bitcast.60, f32[4,1024,512]{2,1,0:T(8,128)S(1)} %fusion.35, f32[4,2048,128]{2,1,0:T(8,128)} %all-gather.14.cloned.1.call-done, s32[]{:T(128)S(6)} %select_n.49), kind=kOutput, calls=%fused_computation.6 | convolution fusion | flops 3223322624 | bytes 18350084 | tf_op jit(solution)/shard_map/src,sck->srk/dot_general | solution.py:10
  352.9 58.3 %all-gather.18.cloned.1.call-done = f32[2,4096,128]{2,1,0:T(8,128)} async-done(((f32[2,512,128]{2,1,0:T(8,128)}), f32[2,4096,128]{2,1,0:T(8,128)}) %all-gather.18.cloned.1.call-update) | async-done | bytes 4194320 | tf_op jit(solution)/shard_map/all_gather | solution.py:40
  411.2 13.7 %fusion.9 = f32[1,1024,128]{2,1,0:T(8,128)} fusion(f32[2,1024,1024]{2,1,0:T(8,128)} %param.20, f32[2,1024,1024]{2,1,0:T(8,128)} %fusion.29, f32[2,4096,128]{2,1,0:T(8,128)} %all-gather.18.cloned.1.call-done, s32[]{:T(128)S(6)} %select_n.52), kind=kOutput, calls=%fused_computation.7 | convolution fusion | flops 3223322624 | bytes 18350084 | tf_op jit(solution)/shard_map/src,sck->srk/dot_general | solution.py:10
  424.8 0.0 all-reduce.6.cloned.1.call-update
  424.8 0.0 all-gather.20.cloned.1.call-start
  424.9 34.5 %all-reduce.6.cloned.1.call-done = (f32[1,1024,128]{2,1,0:T(8,128)}, f32[1,1024,128]{2,1,0:T(8,128)}) async-done(((f32[1,1024,128]{2,1,0:T(8,128)}, f32[1,1024,128]{2,1,0:T(8,128)}), (f32[1,1024,128]{2,1,0:T(8,128)}, f32[1,1024,128]{2,1,0:T(8,128)})) %all-reduce.6.cloned.1.call-update) | async-done | bytes 1048592 | tf_op jit(solution)/shard_map/psum | solution.py:76
  459.4 0.0 copy-done.3
  459.4 2.1 fusion.23
  461.4 0.0 all-gather.20.cloned.1.call-update
  461.5 0.0 all-gather.26.cloned.1.call-start
  461.5 74.6 %all-gather.20.cloned.1.call-done = f32[1,8192,128]{2,1,0:T(8,128)} async-done(((f32[1,1024,128]{2,1,0:T(8,128)}), f32[1,8192,128]{2,1,0:T(8,128)}) %all-gather.20.cloned.1.call-update) | async-done | bytes 4194320 | tf_op jit(solution)/shard_map/all_gather | solution.py:40
  536.1 13.3 %convolution_bitcast_fusion = f32[1024,128]{0,1:T(8,128)} fusion(f32[1024,2048]{1,0:T(8,128)} %param.17, f32[1,8192,128]{2,1,0:T(8,128)} %all-gather.20.cloned.1.call-done, s32[]{:T(128)S(6)} %select_n.55), kind=kOutput, calls=%fused_computation.8 | convolution fusion | flops 3221225472 | bytes 9961476 | tf_op jit(solution)/shard_map/src,sck->srk/dot_general | solution.py:10
  549.5 0.0 all-gather.26.cloned.1.call-update
  549.5 21.0 %all-gather.26.cloned.1.call-done = f32[4096,128]{0,1:T(8,128)} async-done(((f32[1024,128]{0,1:T(8,128)}), f32[4096,128]{0,1:T(8,128)}) %all-gather.26.cloned.1.call-update) | async-done | bytes 2097168 | tf_op jit(solution)/shard_map/all_gather | solution.py:46
  570.5 3.6 reshape.170
  574.1 2.9 reduce.1
  577.0 1.0 copy.40
  578.0 0.0 copy-done.1
  (16 shorter events, 0.1 us)
Async XLA Ops:
  7.2 81.2 %copy-start = (f32[4,256,512]{2,1,0:T(8,128)S(1)}, f32[4,256,512]{2,1,0:T(8,128)}, u32[]{:S(2)}) copy-start(f32[4,256,512]{2,1,0:T(8,128)} %param.15) | copy-start | bytes 6291460
  7.2 81.2 %all-gather.12.cloned.1.call-start = ((), (), s32[]{:S(2)}) async-start(), calls=%async_computation | async-start | bytes 4718592 | tf_op jit(solution)/shard_map/all_gather | solution.py:40
  9.4 104.3 %all-gather.22.cloned.1.call-start = ((), (), s32[]{:S(2)}) async-start(), calls=%async_computation.6 | async-start | bytes 2621440 | tf_op jit(solution)/shard_map/all_gather | solution.py:46
  9.5 106.9 %copy-start.4 = (s32[4,32,16]{1,2,0:T(8,128)S(1)}, s32[4,32,16]{1,2,0:T(8,128)}, u32[]{:S(2)}) copy-start(s32[4,32,16]{1,2,0:T(8,128)} %param.21) | copy-start | bytes 24580
  92.8 97.1 %all-gather.14.cloned.1.call-start = ((), (), s32[]{:S(2)}) async-start(), calls=%async_computation.1 | async-start | bytes 4718592 | tf_op jit(solution)/shard_map/all_gather | solution.py:40
  116.3 113.7 %all-reduce.4.cloned.1.call-start = ((), (), s32[]{:S(2)}) async-start(), calls=%async_computation.2 | async-start | bytes 1048576 | tf_op jit(solution)/shard_map/psum | solution.py:72
  119.3 79.2 %copy-start.2 = (f32[2,512,128]{2,1,0:T(8,128)S(1)}, f32[2,512,128]{2,1,0:T(8,128)}, u32[]{:S(2)}) copy-start(f32[2,512,128]{2,1,0:T(8,128)} %param.13) | copy-start | bytes 1572868
  198.4 107.6 %all-gather.16.cloned.1.call-start = ((), (), s32[]{:S(2)}) async-start(), calls=%async_computation.3 | async-start | bytes 4718592 | tf_op jit(solution)/shard_map/all_gather | solution.py:40
  232.0 103.0 %all-gather.24.cloned.1.call-start = ((), (), s32[]{:S(2)}) async-start(), calls=%async_computation.7 | async-start | bytes 2621440 | tf_op jit(solution)/shard_map/all_gather | solution.py:46
  232.0 105.7 %copy-start.5 = (s32[2,64,32]{1,2,0:T(8,128)S(1)}, s32[2,64,32]{1,2,0:T(8,128)}, u32[]{:S(2)}) copy-start(s32[2,64,32]{1,2,0:T(8,128)} %param.23) | copy-start | bytes 49156
  232.0 105.8 %copy-start.6 = (s32[4,64,16]{1,2,0:T(8,128)S(1)}, s32[4,64,16]{1,2,0:T(8,128)}, u32[]{:S(2)}) copy-start(s32[4,64,16]{1,2,0:T(8,128)} %param.22) | copy-start | bytes 49156
  314.0 97.2 %all-gather.18.cloned.1.call-start = ((), (), s32[]{:S(2)}) async-start(), calls=%async_computation.4 | async-start | bytes 4718592 | tf_op jit(solution)/shard_map/all_gather | solution.py:40
  337.6 121.8 %all-reduce.6.cloned.1.call-start = ((), (), s32[]{:S(2)}) async-start(), calls=%async_computation.9 | async-start | bytes 2097152 | tf_op jit(solution)/shard_map/psum | solution.py:76
  338.2 5.8 slice-start
  339.5 4.6 slice-start.1
  352.9 106.5 %copy-start.3 = (f32[1024,128]{1,0:T(8,128)S(1)}, f32[1024,128]{1,0:T(8,128)}, u32[]{:S(2)}) copy-start(f32[1024,128]{1,0:T(8,128)} %param.14) | copy-start | bytes 1572868
  424.8 111.3 %all-gather.20.cloned.1.call-start = ((), (), s32[]{:S(2)}) async-start(), calls=%async_computation.5 | async-start | bytes 4718592 | tf_op jit(solution)/shard_map/all_gather | solution.py:40
  461.5 109.0 %all-gather.26.cloned.1.call-start = ((), (), s32[]{:S(2)}) async-start(), calls=%async_computation.8 | async-start | bytes 2621440 | tf_op jit(solution)/shard_map/all_gather | solution.py:46
  549.5 28.5 %copy-start.1 = (f32[4,256,512]{2,1,0:T(8,128)S(1)}, f32[4,256,512]{2,1,0:T(8,128)}, u32[]{:S(2)}) copy-start(f32[4,256,512]{2,1,0:T(8,128)} %param.15) | copy-start | bytes 6291460
Sparse Core Ops, SparseCore 0:
  10.6 77.7 all-gather.11
  93.0 20.7 all-gather.21
  116.5 73.3 all-gather.13
  198.6 31.4 all-reduce.3
  232.6 73.3 all-gather.15
  314.1 20.8 all-gather.23
  337.7 73.3 all-gather.17
  425.0 34.3 all-reduce.5
  462.3 73.8 all-gather.19
  549.6 20.8 all-gather.25
